TPU v7x, 128 devices: a whole 4x4x4 slice. The times are simulated.
128 devices in a mesh: dp: 16 (over x, y), expert: 8 (over z, core).
Axes of the slice: x: 4, y: 4, z: 4, core: 2. Of those that a mesh axis runs over, the one named last changes fastest.
Arguments:
- context: bfloat16 [8192, 4096], P('dp'), may hold values from -6 to 6
- out_weight: bfloat16 [4096, 4096], P('dp', 'expert'), may hold values from -0.09375 to 0.09375
- residual: bfloat16 [8192, 4096], P('dp', 'expert'), may hold values from -6 to 6
- gate_weight: bfloat16 [8, 4096, 8192], P('expert', None, 'dp'), may hold values from -0.09375 to 0.09375
- up_weight: bfloat16 [8, 4096, 8192], P('expert', None, 'dp'), may hold values from -0.09375 to 0.09375
- down_weight: bfloat16 [8, 8192, 4096], P('expert', 'dp'), may hold values from -0.0625 to 0.0625
- gate_values: float32 [8, 512], P('expert'), may hold values from 0.2 to 1
- chosen_blocks: int32 [8, 4], replicated, may hold values from 0 to 63, as said below
- block_counts: int32 [8], replicated, may hold values from 1 to 4, as said below
Outputs:
- mixed: bfloat16 [8192, 4096], P('dp', 'expert')
Inputs may be any that keep to these rules, and one draw needn't show every extreme that they name: `chosen_blocks`: within one expert the 4 block numbers are distinct; slots from block_counts on are unused but hold valid block numbers. `block_counts`: some expert uses all 4 slots.
All inputs are finite; a program needn't handle non-finite values.
Results may differ from a plain program's by a relative error of at most 0.008.
Values may be sent and summed in bfloat16 or wider, within the bound.
A program may use at most 128 MiB of HBM per device.

v0:
```python
import jax
import jax.numpy as jnp
from jax import lax
from jax.sharding import PartitionSpec as P

BLK = 128
CAP = 4


def spread_2(value, axis, source):
    kept = jnp.where(lax.axis_index(axis) == source, value, 0).astype(value.dtype)
    return lax.psum(kept, axis)


def spread(selected, owners):
    return jnp.stack(
        [spread_2(selected[slot], "dp", owners[slot]) for slot in range(selected.shape[0])]
    )


def expert_block(inputs, w_gate, w_up, down_split, scale):
    gate = jnp.dot(inputs, w_gate, preferred_element_type=jnp.float32)
    upper = jnp.dot(inputs, w_up, preferred_element_type=jnp.float32)
    hidden = (jax.nn.silu(gate) * upper).astype(jnp.bfloat16)
    part = jnp.einsum("rf,fcd->crd", hidden, down_split, preferred_element_type=jnp.float32)
    return (part * scale[None, :, None]).astype(jnp.bfloat16)


def body(
    context,
    out_weight,
    residual,
    gate_weight,
    up_weight,
    down_weight,
    gate_values,
    chosen_blocks,
    block_counts,
):
    n_expert = lax.axis_size("expert")
    local_tokens = context.shape[0]
    local_width = residual.shape[1]
    model_width = context.shape[1]
    local_blocks = local_tokens // BLK
    my_expert = lax.axis_index("expert")
    my_data = lax.axis_index("dp")
    projected = jnp.dot(
        context,
        lax.all_gather(out_weight, "dp", axis=0, tiled=True),
        preferred_element_type=jnp.float32,
    )
    attended = (residual.astype(jnp.float32) + projected).astype(jnp.bfloat16)
    owners = chosen_blocks // local_blocks
    offsets = chosen_blocks % local_blocks
    my_owners = lax.dynamic_index_in_dim(owners, my_expert, 0, keepdims=False)
    my_offsets = lax.dynamic_index_in_dim(offsets, my_expert, 0, keepdims=False)
    whole = lax.all_gather(attended, "expert", axis=1, tiled=True)
    selected = whole.reshape(local_blocks, BLK, model_width)[my_offsets]
    picked = spread(selected, my_owners).reshape(CAP * BLK, model_width)
    w_gate = gate_weight[0]
    w_up = up_weight[0]
    down_split = down_weight[0].reshape(down_weight.shape[1], n_expert, local_width)
    gate_row = gate_values[0]
    my_count = lax.dynamic_index_in_dim(block_counts, my_expert, 0, keepdims=False)
    live = jnp.arange(CAP * BLK) // BLK < my_count
    scale = jnp.where(live, gate_row, jnp.zeros_like(gate_row))
    partial_value = expert_block(picked, w_gate, w_up, down_split, scale)
    received = lax.all_to_all(partial_value, "expert", split_axis=0, concat_axis=0, tiled=True)
    terms = received.reshape(n_expert * CAP * BLK, local_width).astype(jnp.float32)
    expert_out = lax.psum(terms.astype(jnp.bfloat16), "dp")
    expert_out = expert_out.reshape(n_expert * CAP, BLK, local_width)
    flat_owners = owners.reshape(-1)
    flat_offsets = offsets.reshape(-1)
    selector = (flat_owners[None, :] == my_data) & (
        flat_offsets[None, :] == jnp.arange(local_blocks)[:, None]
    )
    added = jnp.einsum(
        "bs,srd->brd", selector.astype(jnp.bfloat16), expert_out, preferred_element_type=jnp.float32
    )
    total = attended.astype(jnp.float32).reshape(local_blocks, BLK, local_width) + added
    return total.reshape(local_tokens, local_width).astype(jnp.bfloat16)


def solution(mesh):
    in_specs = (
        P("dp", None),
        P("dp", "expert"),
        P("dp", "expert"),
        P("expert", None, "dp"),
        P("expert", None, "dp"),
        P("expert", "dp", None),
        P("expert", None),
        P(),
        P(),
    )
    out_specs = P("dp", "expert")
    return jax.shard_map(body, mesh=mesh, in_specs=in_specs, out_specs=out_specs, check_vma=False)
```

profile of v0, /device:TPU:1, one launch (start us, length us, event | category | flops | bytes accessed | tf_op | source)
XLA Modules:
  0.0 398.1 jit_solution(8035669221233366851)
XLA Ops:
  6.5 0.7 all-gather.3.cloned.1.call-update
  7.3 0.0 all-gather.5.cloned.1.call-start
  7.3 56.8 %all-gather.3.cloned.1.call-done = bf16[4096,512]{1,0:T(8,128)(2,1)} async-done(((bf16[256,512]{1,0:T(8,128)(2,1)}), bf16[4096,512]{1,0:T(8,128)(2,1)}) %all-gather.3.cloned.1.call-update) | async-done | bytes 4194320 | tf_op jit(solution)/shard_map/all_gather | solution.py:49
  64.1 6.6 %fusion.12 = bf16[512,512]{1,0:T(8,128)(2,1)} fusion(bf16[512,4096]{1,0:T(8,128)(2,1)} %param.9, bf16[4096,512]{1,0:T(8,128)(2,1)} %all-gather.3.cloned.1.call-done, bf16[512,512]{1,0:T(8,128)(2,1)} %param.11), kind=kOutput, calls=%fused_computation.12 | convolution fusion | flops 2148270080 | bytes 9437184 | tf_op jit(solution)/shard_map/dot_general | solution.py:47
  70.8 0.0 all-gather.5.cloned.1.call-update
  70.8 0.0 all-reduce.6.cloned.1.call-start
  70.9 0.2 dynamic-slice_reduce_fusion
  71.1 0.6 fusion.33
  74.3 29.1 %all-gather.5.cloned.1.call-done = bf16[512,4096]{1,0:T(8,128)(2,1)} async-done(((bf16[512,512]{1,0:T(8,128)(2,1)}), bf16[512,4096]{1,0:T(8,128)(2,1)}) %all-gather.5.cloned.1.call-update) | async-done | bytes 4194320 | tf_op jit(solution)/shard_map/all_gather | solution.py:57
  103.4 5.0 %gather_fusion = bf16[4,128,4096]{2,1,0:T(8,128)(2,1)} fusion(bf16[4,128,4096]{2,1,0:T(8,128)(2,1)} %bitcast.46, s32[1024]{0:T(1024)S(1)} %pad_clamp_fusion), kind=kCustom, calls=%fused_computation | custom fusion | bytes 8388624 | tf_op jit(solution)/shard_map/gather | solution.py:58
  108.4 4.2 %slice_select_fusion.3 = (bf16[1,128,4096]{2,1,0:T(8,128)(2,1)}, bf16[1,128,4096]{2,1,0:T(8,128)(2,1)}, bf16[1,128,4096]{2,1,0:T(8,128)(2,1)}, bf16[1,128,4096]{2,1,0:T(8,128)(2,1)}) fusion(bf16[4,128,4096]{2,1,0:T(8,128)(2,1)} %gather_fusion, pred[]{:T(512)S(6)} %eq.50, pred[]{:T(512)S(6)} %eq.52, pred[]{:T(512)S(6)} %eq.51, pred[]{:T(512)S(6)} %eq.53), kind=kLoop, calls=%fused_computation.18 | loop fusion | flops 2097152 | bytes 8388612 | tf_op jit(solution)/shard_map/jit(_where)/select_n | solution.py:11
  112.6 0.0 all-reduce.6.cloned.1.call-update
  112.6 0.0 all-reduce.4.cloned.1.call-start
  112.7 0.6 copy-done.6
  113.3 0.6 dynamic_slice.13
  113.9 6.4 %copy.26 = bf16[64,8,8,512]{3,2,1,0:T(8,128)(2,1)} copy(bf16[64,8,8,512]{3,1,2,0:T(8,128)(2,1)} %bitcast.45) | data formatting | bytes 8388608
  120.3 0.6 fusion.23
  120.9 95.0 %all-reduce.6.cloned.1.call-done = (bf16[1,128,4096]{2,1,0:T(8,128)(2,1)}, bf16[1,128,4096]{2,1,0:T(8,128)(2,1)}, bf16[1,128,4096]{2,1,0:T(8,128)(2,1)}, bf16[1,128,4096]{2,1,0:T(8,128)(2,1)}) async-done(((bf16[1,128,4096]{2,1,0:T(8,128)(2,1)}, bf16[1,128,4096]{2,1,0:T(8,128)(2,1)}, bf16[1,128,4096]{2,1,0:T(8,128)(2,1)}, bf16[1,128,4096]{2,1,0:T(8,128)(2,1)}), (bf16[1,128,4096]{2,1,0:T(8,128)(2,1)}, ...) | async-done | bytes 4194320 | tf_op jit(solution)/shard_map/psum | solution.py:12
  215.9 2.6 pad_maximum_fusion
  218.5 0.9 copy-done.4
  219.4 2.3 fusion.3
  221.7 2.4 fusion.16
  224.1 3.4 fusion
  227.5 54.3 %all_to_all.5 = bf16[8,512,512]{2,1,0:T(8,128)(2,1)S(1)} all-to-all(bf16[8,512,512]{2,1,0:T(8,128)(2,1)S(1)} %fusion), channel_id=1, replica_groups=mesh['dp'=16,'expert'=8] {'expert'}, dimensions={0} | all-to-all | bytes 8388608 | tf_op jit(solution)/shard_map/all_to_all | solution.py:68
  281.8 4.4 %copy.24 = bf16[32,128,512]{2,0,1:T(8,128)(2,1)} copy(bf16[32,128,512]{2,1,0:T(8,128)(2,1)S(1)} %bitcast.44) | data formatting | bytes 8388608 | tf_op jit(solution)/shard_map/reshape | solution.py:71
  286.2 0.1 copy.22
  286.3 0.1 copy.21
  286.4 0.1 eq.45
  286.5 0.1 eq.46
  286.6 101.1 %all-reduce.4.cloned.1.call-done = bf16[32,128,512]{2,0,1:T(8,128)(2,1)} async-done(((bf16[32,128,512]{2,0,1:T(8,128)(2,1)}), bf16[32,128,512]{2,0,1:T(8,128)(2,1)}) %all-reduce.4.cloned.1.call-update) | async-done | bytes 4194320 | tf_op jit(solution)/shard_map/psum | solution.py:70
  387.6 2.8 fusion.28
  390.5 1.1 fusion.19
  (18 shorter events, 0.1 us)
Async XLA Ops:
  6.5 57.6 %all-gather.3.cloned.1.call-start = ((), (), s32[]{:S(2)}) async-start(), calls=%async_computation.1 | async-start | bytes 4456448 | tf_op jit(solution)/shard_map/all_gather | solution.py:49
  7.3 63.6 %copy-start.2 = (s32[8,4]{0,1:T(4,128)S(1)}, s32[8,4]{0,1:T(4,128)}, u32[]{:S(2)}) copy-start(s32[8,4]{0,1:T(4,128)} %param.16) | copy-start | bytes 388
  7.3 96.1 %all-gather.5.cloned.1.call-start = ((), (), s32[]{:S(2)}) async-start(), calls=%async_computation.2 | async-start | bytes 4718592 | tf_op jit(solution)/shard_map/all_gather | solution.py:57
  70.8 145.1 %all-reduce.6.cloned.1.call-start = ((), (), s32[]{:S(2)}) async-start(), calls=%async_computation.4 | async-start | bytes 8388608 | tf_op jit(solution)/shard_map/psum | solution.py:12
  112.6 0.7 copy-start.6
  112.6 275.0 %all-reduce.4.cloned.1.call-start = ((), (), s32[]{:S(2)}) async-start(), calls=%async_computation.3 | async-start | bytes 8388608 | tf_op jit(solution)/shard_map/psum | solution.py:70
  113.9 6.4 %copy-start.3 = (f32[1,512]{1,0:T(1,128)S(1)}, f32[1,512]{1,0:T(1,128)}, u32[]{:S(2)}) copy-start(f32[1,512]{1,0:T(1,128)} %param.15) | copy-start | bytes 6148
  215.9 3.4 copy-start.4
  219.4 2.3 copy-start.5
  221.7 2.4 copy-start
  286.2 104.3 %copy-start.1 = (bf16[512,512]{1,0:T(8,128)(2,1)S(1)}, bf16[512,512]{1,0:T(8,128)(2,1)}, u32[]{:S(2)}) copy-start(bf16[512,512]{1,0:T(8,128)(2,1)} %fusion.12) | copy-start | bytes 1572868
Sparse Core Ops, SparseCore 0:
  9.5 54.5 all-gather.2
  70.9 32.4 all-gather.4
  112.7 103.1 all-reduce.5
  286.4 101.2 all-reduce.3
where the time goes:
time: 398 us
  waiting for transfers between devices  283 us (71%)
  blocking collectives  54.3 us (14%)
  local copies, waits for them, and re-layouts  19 us (5%)
  matrix products  17.6 us (4%)
  between operations  15.8 us (4%)
  other arithmetic  8.58 us (2%)
    psum x1, waiting for transfers between devices, body(): expert_out = lax.psum(terms.astype(jnp.bfloat16), 'dp')  101 us
    psum x1, waiting for transfers between devices, spread_2(): return lax.psum(kept, axis)  95 us
    all_gather x1, waiting for transfers between devices, body(): lax.all_gather(out_weight, 'dp', axis=0, tiled=True)  56.8 us
    all_to_all x1, blocking collectives, body(): lax.all_to_all(partial_value, 'expert', split_axis=0, concat_axis=0, tile...  54.3 us
    all_gather x1, waiting for transfers between devices, body(): whole = lax.all_gather(attended, 'expert', axis=1, tiled=True)  29.1 us
  transfers between devices with their start and end apart: 4, of which 4 were waited for; matrix products, arithmetic and copies ran while one was open for 2% of the time, Pallas kernels for 0%

commit v1 on v0

--- a/solution.py
+++ b/solution.py
@@ -9,7 +9,7 @@
 
 def spread_2(value, axis, source):
     kept = jnp.where(lax.axis_index(axis) == source, value, 0).astype(value.dtype)
-    return lax.psum(kept, axis)
+    return jnp.sum(lax.all_gather(kept, axis), axis=0)
 
 
 def spread(selected, owners):

time: 398 us -> 754 us (1.89)
  waiting for transfers between devices: 283 us -> 602 us
  other arithmetic: 8.58 us -> 44.4 us
    all_gather x0 -> x4, waiting for transfers between devices: none -> 413 us  [spread_2(): return jnp.sum(lax.all_gather(kept, axis), axis=0)]
    psum x1 -> x0, waiting for transfers between devices: 95 us -> none  [spread_2(): return lax.psum(kept, axis)]
    reduce_sum x0 -> x4, other arithmetic: none -> 36.7 us  [spread_2(): return jnp.sum(lax.all_gather(kept, axis), axis=0)]
  transfers between devices with their start and end apart: 4 -> 7, of which waited for: 4 -> 7; matrix products, arithmetic and copies ran while one was open for 2% -> 5% of each run, Pallas kernels for 0% -> 0%
where the time goes in v1:
time: 754 us
  waiting for transfers between devices  602 us (80%)
  blocking collectives  54.2 us (7%)
  other arithmetic  44.4 us (6%)
  local copies, waits for them, and re-layouts  18.3 us (2%)
  matrix products  17.6 us (2%)
  between operations  16.1 us (2%)
    all_gather x4, waiting for transfers between devices, spread_2(): return jnp.sum(lax.all_gather(kept, axis), axis=0)  413 us
    psum x1, waiting for transfers between devices, body(): expert_out = lax.psum(terms.astype(jnp.bfloat16), 'dp')  101 us
    all_gather x1, waiting for transfers between devices, body(): lax.all_gather(out_weight, 'dp', axis=0, tiled=True)  56.8 us
    all_to_all x1, blocking collectives, body(): lax.all_to_all(partial_value, 'expert', split_axis=0, concat_axis=0, tile...  54.2 us
    reduce_sum x4, other arithmetic, spread_2(): return jnp.sum(lax.all_gather(kept, axis), axis=0)  36.7 us
    all_gather x1, waiting for transfers between devices, body(): whole = lax.all_gather(attended, 'expert', axis=1, tiled=True)  29.3 us
  transfers between devices with their start and end apart: 7, of which 7 were waited for; matrix products, arithmetic and copies ran while one was open for 5% of the time, Pallas kernels for 0%

profile of v1, /device:TPU:1, one launch (start us, length us, event | category | flops | bytes accessed | tf_op | source)
XLA Modules:
  0.0 753.5 jit_solution(11670754064154414247)
XLA Ops:
  6.5 0.7 all-gather.7.cloned.1.call-update
  7.3 56.8 %all-gather.7.cloned.1.call-done = bf16[4096,512]{1,0:T(8,128)(2,1)} async-done(((bf16[256,512]{1,0:T(8,128)(2,1)}), bf16[4096,512]{1,0:T(8,128)(2,1)}) %all-gather.7.cloned.1.call-update) | async-done | bytes 4194320 | tf_op jit(solution)/shard_map/all_gather | solution.py:49
  64.1 6.6 fusion.12
  71.1 0.6 fusion.33
  74.1 29.3 %all-gather.9.cloned.1.call-done = bf16[512,4096]{1,0:T(8,128)(2,1)} async-done(((bf16[512,512]{1,0:T(8,128)(2,1)}), bf16[512,4096]{1,0:T(8,128)(2,1)}) %all-gather.9.cloned.1.call-update) | async-done | bytes 4194320 | tf_op jit(solution)/shard_map/all_gather | solution.py:57
  103.4 5.0 gather_fusion
  108.4 4.2 slice_select_fusion.3
  112.7 0.5 all-gather.15.cloned.1.call-update
  113.2 0.5 all-gather.13.cloned.1.call-update
  113.8 0.5 all-gather.17.cloned.1.call-update
  114.4 0.2 all-reduce.2.cloned.1.call-start
  114.6 0.6 dynamic_slice.13
  115.2 6.4 copy.32
  121.7 0.6 fusion.23
  122.3 101.0 %all-gather.11.cloned.1.call-done = bf16[16,128,4096]{2,1,0:T(8,128)(2,1)} async-done(((bf16[1,128,4096]{2,1,0:T(8,128)(2,1)}), bf16[16,128,4096]{2,1,0:T(8,128)(2,1)}) %all-gather.11.cloned.1.call-update) | async-done | bytes 16777232 | tf_op jit(solution)/shard_map/all_gather | solution.py:12
  223.3 8.9 %reduce_sum.48 = bf16[128,4096]{1,0:T(8,128)(2,1)S(1)} reduce(bf16[16,128,4096]{2,1,0:T(8,128)(2,1)} %all-gather.11.cloned.1.call-done, bf16[]{:T(256)} %constant.73.clone.1), dimensions={0}, to_apply=%region_0.1 | reduce | flops 7864320 | bytes 17825794 | tf_op jit(solution)/shard_map/reduce_sum | solution.py:12
  232.2 104.0 %all-gather.15.cloned.1.call-done = bf16[16,128,4096]{2,1,0:T(8,128)(2,1)} async-done(((bf16[1,128,4096]{2,1,0:T(8,128)(2,1)}), bf16[16,128,4096]{2,1,0:T(8,128)(2,1)}) %all-gather.15.cloned.1.call-update) | async-done | bytes 16777232 | tf_op jit(solution)/shard_map/all_gather | solution.py:12
  336.2 8.9 %reduce_sum.50 = bf16[128,4096]{1,0:T(8,128)(2,1)S(1)} reduce(bf16[16,128,4096]{2,1,0:T(8,128)(2,1)} %all-gather.15.cloned.1.call-done, bf16[]{:T(256)} %constant.73.clone.1), dimensions={0}, to_apply=%region_2.3 | reduce | flops 7864320 | bytes 17825794 | tf_op jit(solution)/shard_map/reduce_sum | solution.py:12
  345.2 104.0 %all-gather.13.cloned.1.call-done = bf16[16,128,4096]{2,1,0:T(8,128)(2,1)} async-done(((bf16[1,128,4096]{2,1,0:T(8,128)(2,1)}), bf16[16,128,4096]{2,1,0:T(8,128)(2,1)}) %all-gather.13.cloned.1.call-update) | async-done | bytes 16777232 | tf_op jit(solution)/shard_map/all_gather | solution.py:12
  449.2 8.9 %reduce_sum.49 = bf16[128,4096]{1,0:T(8,128)(2,1)S(1)} reduce(bf16[16,128,4096]{2,1,0:T(8,128)(2,1)} %all-gather.13.cloned.1.call-done, bf16[]{:T(256)} %constant.73.clone.1), dimensions={0}, to_apply=%region_1.2 | reduce | flops 7864320 | bytes 17825794 | tf_op jit(solution)/shard_map/reduce_sum | solution.py:12
  458.1 104.0 %all-gather.17.cloned.1.call-done = bf16[16,128,4096]{2,1,0:T(8,128)(2,1)} async-done(((bf16[1,128,4096]{2,1,0:T(8,128)(2,1)}), bf16[16,128,4096]{2,1,0:T(8,128)(2,1)}) %all-gather.17.cloned.1.call-update) | async-done | bytes 16777232 | tf_op jit(solution)/shard_map/all_gather | solution.py:12
  562.1 9.9 %reduce_sum.51 = bf16[128,4096]{1,0:T(8,128)(2,1)} reduce(bf16[16,128,4096]{2,1,0:T(8,128)(2,1)} %all-gather.17.cloned.1.call-done, bf16[]{:T(256)} %constant.73.clone.1), dimensions={0}, to_apply=%region_3.4 | reduce | flops 7864320 | bytes 17825794 | tf_op jit(solution)/shard_map/reduce_sum | solution.py:12
  572.0 1.7 pad_maximum_fusion
  573.8 0.7 copy-done.4
  574.5 2.3 fusion.3
  576.9 2.4 fusion.16
  579.3 3.4 fusion
  582.7 54.2 %all_to_all.5 = bf16[8,512,512]{2,1,0:T(8,128)(2,1)S(1)} all-to-all(bf16[8,512,512]{2,1,0:T(8,128)(2,1)S(1)} %fusion), channel_id=1, replica_groups=mesh['dp'=16,'expert'=8] {'expert'}, dimensions={0} | all-to-all | bytes 8388608 | tf_op jit(solution)/shard_map/all_to_all | solution.py:68
  636.9 4.4 copy.30
  641.7 101.0 %all-reduce.2.cloned.1.call-done = bf16[32,128,512]{2,0,1:T(8,128)(2,1)} async-done(((bf16[32,128,512]{2,0,1:T(8,128)(2,1)}), bf16[32,128,512]{2,0,1:T(8,128)(2,1)}) %all-reduce.2.cloned.1.call-update) | async-done | bytes 4194320 | tf_op jit(solution)/shard_map/psum | solution.py:70
  742.7 2.8 fusion.28
  745.5 1.1 fusion.19
  (31 shorter events, 0.8 us)
Async XLA Ops:
  6.5 57.6 %all-gather.7.cloned.1.call-start = ((), (), s32[]{:S(2)}) async-start(), calls=%async_computation.1 | async-start | bytes 4456448 | tf_op jit(solution)/shard_map/all_gather | solution.py:49
  7.3 63.6 %copy-start.2 = (s32[8,4]{0,1:T(4,128)S(1)}, s32[8,4]{0,1:T(4,128)}, u32[]{:S(2)}) copy-start(s32[8,4]{0,1:T(4,128)} %param.16) | copy-start | bytes 388
  7.3 96.1 %all-gather.9.cloned.1.call-start = ((), (), s32[]{:S(2)}) async-start(), calls=%async_computation.2 | async-start | bytes 4718592 | tf_op jit(solution)/shard_map/all_gather | solution.py:57
  70.8 152.5 %all-gather.11.cloned.1.call-start = ((), (), s32[]{:S(2)}) async-start(), calls=%async_computation.3 | async-start | bytes 17825792 | tf_op jit(solution)/shard_map/all_gather | solution.py:12
  112.6 2.0 copy-start.6
  112.6 223.6 %all-gather.15.cloned.1.call-start = ((), (), s32[]{:S(2)}) async-start(), calls=%async_computation.5 | async-start | bytes 17825792 | tf_op jit(solution)/shard_map/all_gather | solution.py:12
  113.2 336.0 %all-gather.13.cloned.1.call-start = ((), (), s32[]{:S(2)}) async-start(), calls=%async_computation.4 | async-start | bytes 17825792 | tf_op jit(solution)/shard_map/all_gather | solution.py:12
  113.8 448.3 %all-gather.17.cloned.1.call-start = ((), (), s32[]{:S(2)}) async-start(), calls=%async_computation.6 | async-start | bytes 17825792 | tf_op jit(solution)/shard_map/all_gather | solution.py:12
  114.4 628.3 %all-reduce.2.cloned.1.call-start = ((), (), s32[]{:S(2)}) async-start(), calls=%async_computation.7 | async-start | bytes 8388608 | tf_op jit(solution)/shard_map/psum | solution.py:70
  115.2 6.4 copy-start.3
  572.0 2.5 copy-start.4
  574.5 2.3 copy-start.5
  576.9 2.4 copy-start
  641.3 104.2 %copy-start.1 = (bf16[512,512]{1,0:T(8,128)(2,1)S(1)}, bf16[512,512]{1,0:T(8,128)(2,1)}, u32[]{:S(2)}) copy-start(bf16[512,512]{1,0:T(8,128)(2,1)} %fusion.12) | copy-start | bytes 1572868
Sparse Core Ops, SparseCore 0:
  9.5 54.5 all-gather.6
  70.9 32.4 all-gather.8
  112.7 110.5 all-gather.10
  225.3 110.8 all-gather.14
  338.2 110.8 all-gather.12
  451.2 110.8 all-gather.16
  641.4 101.1 all-reduce.1
